TPU v7x, 32 devices: a whole 2x2x4 slice. The times are simulated.
32 devices in a mesh: mem: 8 (over z, y), band: 4 (over x, core).
Axes of the slice: x: 2, y: 2, z: 4, core: 2. Of those that a mesh axis runs over, the one named last changes fastest.
Arguments:
- ensemble: float32 [256, 256, 256], P('mem', 'band'), may hold values from -8 to 8
- column_operator: float32 [128, 128], replicated, may hold values from -0.5 to 0.5
- patch_order: int32 [4, 64], P('band'), may hold values from 0 to 63, as said below
- obs_index: int32 [4, 64, 512], P('band'), may hold values from 0 to 255
- obs_count: int32 [4, 64], P('band', 'mem'), may hold values from 1 to 512
- obs_values: float32 [4, 64, 512], P('band', 'mem'), may hold values from -8 to 8
- obs_precision: float32 [4, 64, 512], P('band', 'mem'), may hold values from 2 to 50
Outputs:
- analysis: float32 [256, 256, 256], P('mem', 'band')
- transform: float32 [4, 64, 256, 256], P('band', 'mem')
Inputs may be any that keep to these rules, and one draw needn't show every extreme that they name: `patch_order`: each row is a permutation of 0 to 63.
All inputs are finite; a program needn't handle non-finite values.
Results may differ from a plain program's by a relative error of at most 0.0003.
Values sent between devices are 32-bit elements; how exact they have to be, the bound alone decides.
A program may use at most 64 MiB of HBM per device.

v0:
```python
import math

import jax
import jax.numpy as jnp
from jax import lax
from jax.sharding import PartitionSpec as P

ITERS = 12


def batched(left, right):
    return jnp.einsum("pij,pjk->pik", left, right, precision=lax.Precision.HIGHEST)


def map_columns(states, column_operator):
    rows, patches, cells = states.shape
    levels = column_operator.shape[0]
    flat_rows = states.reshape(rows * patches * (cells // levels), levels)
    mapped = jnp.dot(flat_rows, column_operator, precision=lax.Precision.HIGHEST)
    return mapped.reshape(rows, patches, -1)


def select_slots(channel_values, index):
    width = channel_values.shape[2]
    places = jnp.arange(width, dtype=jnp.int32)
    picker = (index[:, None, :] == places[None, :, None]).astype(jnp.float32)
    return jnp.einsum("kpc,pco->kpo", channel_values, picker, precision=lax.Precision.HIGHEST)


def local(ensemble, column_operator, patch_order, obs_index, obs_count, obs_values, obs_precision):
    highest = lax.Precision.HIGHEST
    members_dev, band_patches, cells = ensemble.shape
    slots = obs_index.shape[2]
    n_mem = lax.axis_size("mem")
    worker = lax.axis_index("mem")
    per_worker = band_patches // n_mem
    order = patch_order[0]
    positions = jnp.arange(band_patches, dtype=jnp.int32)
    permuter = (order[None, :] == positions[:, None]).astype(jnp.float32)
    listed = jnp.einsum("kqc,qj->kjc", ensemble, permuter, precision=highest)
    my_index = lax.dynamic_slice_in_dim(obs_index[0], worker * per_worker, per_worker, 0)
    state_in = lax.all_to_all(listed, "mem", split_axis=1, concat_axis=0, tiled=True)
    obs_block = select_slots(map_columns(state_in, column_operator), my_index)
    count = obs_count[0]
    values = obs_values[0]
    precision = obs_precision[0]
    members = obs_block.shape[0]
    live = (jnp.arange(slots, dtype=jnp.int32)[None, :] < count[:, None]).astype(jnp.float32)
    obs_weight = precision * live
    obs_mean = jnp.mean(obs_block, axis=0)
    obs_pert = obs_block - obs_mean
    innov = (values - obs_mean) * obs_weight
    gram = jnp.einsum("kpo,jpo->pkj", obs_pert * obs_weight, obs_pert, precision=highest)
    identity = jnp.eye(members, dtype=jnp.float32)
    system = gram + (members - 1.0) * identity
    trace_value = jnp.trace(system, axis1=1, axis2=2)
    level = system / trace_value[:, None, None]

    def sweep(step, carry):
        ymat, zmat = carry
        turn = 1.5 * identity - 0.5 * batched(zmat, ymat)
        return (batched(ymat, turn), batched(turn, zmat))

    ymat, zmat = lax.fori_loop(0, ITERS, sweep, (level, jnp.broadcast_to(identity, level.shape)))
    root = zmat / jnp.sqrt(trace_value)[:, None, None]
    spread = math.sqrt(members - 1.0) * root
    projected = jnp.einsum("kpo,po->pk", obs_pert, innov, precision=highest)
    inner = jnp.einsum("pij,pj->pi", root, projected, precision=highest)
    mean_weight = jnp.einsum("pij,pj->pi", root, inner, precision=highest)
    coef = spread + mean_weight[:, :, None]
    state_mean = jnp.mean(state_in, axis=0)
    state_pert = state_in - state_mean
    updated = state_mean + jnp.einsum("pjk,jpc->kpc", coef, state_pert, precision=highest)
    returned = lax.all_to_all(updated, "mem", split_axis=0, concat_axis=1, tiled=True)
    restored = jnp.einsum("kjc,qj->kqc", returned, permuter, precision=highest)
    return (restored, spread[None])


def solution(mesh):
    placed = (
        P("mem", "band", None),
        P(),
        P("band", None),
        P("band", None, None),
        P("band", "mem"),
        P("band", "mem", None),
        P("band", "mem", None),
    )
    return jax.shard_map(
        local,
        mesh=mesh,
        in_specs=placed,
        out_specs=(P("mem", "band", None), P("band", "mem", None, None)),
        check_vma=False,
    )
```

profile of v0, /device:TPU:24, one launch (start us, length us, event | category | flops | bytes accessed | tf_op | source)
XLA Modules:
  0.0 325.5 jit_solution(8018955491535311315)
XLA Ops:
  2.2 1.9 convolution_bitcast_fusion
  4.1 2.5 copy.41
  6.7 6.2 %all-to-all-start = ((f32[32,64,256]{2,0,1:T(8,128)}), f32[32,64,256]{2,0,1:T(8,128)}, u32[]{:S(2)}, u32[]{:S(2)}) async-start(f32[32,64,256]{2,0,1:T(8,128)} %copy.41), calls=%async_computation | async-start | bytes 4194304 | tf_op jit(solution)/shard_map/all_to_all | solution.py:42
  13.7 45.9 %all-to-all-done = f32[32,64,256]{2,0,1:T(8,128)} async-done(((f32[32,64,256]{2,0,1:T(8,128)}), f32[32,64,256]{2,0,1:T(8,128)}, u32[]{:S(2)}, u32[]{:S(2)}) %all-to-all-start) | async-done | bytes 2097184 | tf_op jit(solution)/shard_map/all_to_all | solution.py:42
  59.6 4.1 %copy.43 = f32[8,32,8,256]{3,2,1,0:T(8,128)} copy(f32[8,32,8,256]{3,1,2,0:T(8,128)} %bitcast.7) | data formatting | bytes 4194304 | tf_op jit(solution)/shard_map/all_to_all | solution.py:42
  63.8 2.7 bitcast_reduce_fusion.1
  66.4 2.6 reshape.71
  69.1 3.2 bitcast_subtract_fusion.3
  72.3 3.1 fusion.53
  75.4 2.9 reshape.72
  78.3 4.3 %bitcast_reduce_fusion = (f32[8,512]{1,0:T(8,128)S(1)}, f32[8,512,256]{1,2,0:T(8,128)S(1)}) fusion(f32[256,8,256]{2,1,0:T(8,128)} %reshape.72, s32[8,512]{1,0:T(8,128)S(1)} %dynamic-slice_bitcast_fusion), kind=kOutput, calls=%fused_computation.16 | convolution fusion | flops 3223318528 | bytes 6324224 | tf_op jit(solution)/shard_map/kpc,pco->kpo/dot_general | solution.py:27
  82.7 3.7 %fusion.15 = f32[8,1,256]{2,1,0:T(1,128)S(1)} fusion(f32[8,512,256]{1,2,0:T(8,128)S(1)} %get-tuple-element.54, f32[8,512]{1,0:T(8,128)S(1)} %get-tuple-element.52, f32[8,512,1]{1,0,2:T(8,128)S(1)} %get-tuple-element.51), kind=kOutput, calls=%fused_computation.19 | convolution fusion | flops 13631488 | bytes 4235264 | tf_op jit(solution)/shard_map/kpo,po->pk/dot_general | solution.py:67
  86.4 4.7 %select_reduce_fusion = (f32[8]{0:T(128)S(1)}, f32[8,256,256]{2,1,0:T(8,128)S(1)}) fusion(f32[256,256]{1,0:T(8,128)S(1)} %fusion.38, pred[256,256]{1,0:T(8,128)(4,1)S(1)} %iota_compare_fusion.3, f32[8,512,256]{1,2,0:T(8,128)S(1)} %get-tuple-element.54, f32[8,512]{1,0:T(8,128)S(1)} %get-tuple-element.52, f32[8,512]{1,0:T(8,128)S(1)} %select_bitcast_fusion), kind=kOutput, calls=%fused_computation.30 | convolution fusion | flops 3225944064 | bytes 6651936 | tf_op jit(solution)/shard_map/kpo,jpo->pkj/dot_general | solution.py:53
  92.8 2.9 copy.46
  97.2 157.3 %while.13 = (s32[]{:T(128)}, f32[8,256,256]{1,2,0:T(8,128)}, f32[8,256,256]{2,1,0:T(8,128)}, s32[]{:T(128)}) while((s32[]{:T(128)}, f32[8,256,256]{1,2,0:T(8,128)}, f32[8,256,256]{2,1,0:T(8,128)}, s32[]{:T(128)}) %tuple.32), condition=%wide.region_4.5_spmd.clone, body=%wide.region_3.4_spmd.clone.sunk | while | flops 4834066432 | bytes 36438096 | solution.py:64
  97.2 1.7 copy.103
  99.7 2.2 fusion.73
  101.8 4.9 %fusion.75 = f32[8,256,256]{1,2,0:T(8,128)} fusion(f32[8,256,256]{1,2,0:T(8,128)S(1)} %copy.103, f32[8,256,256]{2,1,0:T(8,128)S(1)} %fusion.73, f32[256,256]{1,0:T(8,128)S(1)} %fusion.74), kind=kOutput, calls=%fused_computation.4.clone.1 | convolution fusion | flops 1611661312 | bytes 6553600 | tf_op jit(solution)/shard_map/while/body/eval_jaxpr/pij,pjk->pik/dot_general | solution.py:12
  106.8 3.6 %fusion.76 = f32[8,256,256]{2,1,0:T(8,128)} fusion(f32[8,256,256]{2,1,0:T(8,128)S(1)} %copy.104, f32[8,256,256]{2,1,0:T(8,128)S(1)} %fusion.73, f32[256,256]{1,0:T(8,128)S(1)} %fusion.74), kind=kOutput, calls=%fused_computation.2.clone.1 | convolution fusion | flops 1611661312 | bytes 6553600 | tf_op jit(solution)/shard_map/while/body/eval_jaxpr/pij,pjk->pik/dot_general | solution.py:12
  110.3 1.7 copy.103
  112.8 2.2 fusion.73
  115.0 4.9 %fusion.75 = f32[8,256,256]{1,2,0:T(8,128)} fusion(f32[8,256,256]{1,2,0:T(8,128)S(1)} %copy.103, f32[8,256,256]{2,1,0:T(8,128)S(1)} %fusion.73, f32[256,256]{1,0:T(8,128)S(1)} %fusion.74), kind=kOutput, calls=%fused_computation.4.clone.1 | convolution fusion | flops 1611661312 | bytes 6553600 | tf_op jit(solution)/shard_map/while/body/eval_jaxpr/pij,pjk->pik/dot_general | solution.py:12
  119.9 3.6 %fusion.76 = f32[8,256,256]{2,1,0:T(8,128)} fusion(f32[8,256,256]{2,1,0:T(8,128)S(1)} %copy.104, f32[8,256,256]{2,1,0:T(8,128)S(1)} %fusion.73, f32[256,256]{1,0:T(8,128)S(1)} %fusion.74), kind=kOutput, calls=%fused_computation.2.clone.1 | convolution fusion | flops 1611661312 | bytes 6553600 | tf_op jit(solution)/shard_map/while/body/eval_jaxpr/pij,pjk->pik/dot_general | solution.py:12
  123.4 1.7 copy.103
  125.9 2.2 fusion.73
  128.1 4.9 %fusion.75 = f32[8,256,256]{1,2,0:T(8,128)} fusion(f32[8,256,256]{1,2,0:T(8,128)S(1)} %copy.103, f32[8,256,256]{2,1,0:T(8,128)S(1)} %fusion.73, f32[256,256]{1,0:T(8,128)S(1)} %fusion.74), kind=kOutput, calls=%fused_computation.4.clone.1 | convolution fusion | flops 1611661312 | bytes 6553600 | tf_op jit(solution)/shard_map/while/body/eval_jaxpr/pij,pjk->pik/dot_general | solution.py:12
  133.0 3.6 %fusion.76 = f32[8,256,256]{2,1,0:T(8,128)} fusion(f32[8,256,256]{2,1,0:T(8,128)S(1)} %copy.104, f32[8,256,256]{2,1,0:T(8,128)S(1)} %fusion.73, f32[256,256]{1,0:T(8,128)S(1)} %fusion.74), kind=kOutput, calls=%fused_computation.2.clone.1 | convolution fusion | flops 1611661312 | bytes 6553600 | tf_op jit(solution)/shard_map/while/body/eval_jaxpr/pij,pjk->pik/dot_general | solution.py:12
  136.5 1.7 copy.103
  139.0 2.2 fusion.73
  141.2 4.9 %fusion.75 = f32[8,256,256]{1,2,0:T(8,128)} fusion(f32[8,256,256]{1,2,0:T(8,128)S(1)} %copy.103, f32[8,256,256]{2,1,0:T(8,128)S(1)} %fusion.73, f32[256,256]{1,0:T(8,128)S(1)} %fusion.74), kind=kOutput, calls=%fused_computation.4.clone.1 | convolution fusion | flops 1611661312 | bytes 6553600 | tf_op jit(solution)/shard_map/while/body/eval_jaxpr/pij,pjk->pik/dot_general | solution.py:12
  146.1 3.6 %fusion.76 = f32[8,256,256]{2,1,0:T(8,128)} fusion(f32[8,256,256]{2,1,0:T(8,128)S(1)} %copy.104, f32[8,256,256]{2,1,0:T(8,128)S(1)} %fusion.73, f32[256,256]{1,0:T(8,128)S(1)} %fusion.74), kind=kOutput, calls=%fused_computation.2.clone.1 | convolution fusion | flops 1611661312 | bytes 6553600 | tf_op jit(solution)/shard_map/while/body/eval_jaxpr/pij,pjk->pik/dot_general | solution.py:12
  152.1 2.2 fusion.73
  154.3 4.9 %fusion.75 = f32[8,256,256]{1,2,0:T(8,128)} fusion(f32[8,256,256]{1,2,0:T(8,128)S(1)} %copy.103, f32[8,256,256]{2,1,0:T(8,128)S(1)} %fusion.73, f32[256,256]{1,0:T(8,128)S(1)} %fusion.74), kind=kOutput, calls=%fused_computation.4.clone.1 | convolution fusion | flops 1611661312 | bytes 6553600 | tf_op jit(solution)/shard_map/while/body/eval_jaxpr/pij,pjk->pik/dot_general | solution.py:12
  159.2 3.6 %fusion.76 = f32[8,256,256]{2,1,0:T(8,128)} fusion(f32[8,256,256]{2,1,0:T(8,128)S(1)} %copy.104, f32[8,256,256]{2,1,0:T(8,128)S(1)} %fusion.73, f32[256,256]{1,0:T(8,128)S(1)} %fusion.74), kind=kOutput, calls=%fused_computation.2.clone.1 | convolution fusion | flops 1611661312 | bytes 6553600 | tf_op jit(solution)/shard_map/while/body/eval_jaxpr/pij,pjk->pik/dot_general | solution.py:12
  165.2 2.2 fusion.73
  167.4 4.9 %fusion.75 = f32[8,256,256]{1,2,0:T(8,128)} fusion(f32[8,256,256]{1,2,0:T(8,128)S(1)} %copy.103, f32[8,256,256]{2,1,0:T(8,128)S(1)} %fusion.73, f32[256,256]{1,0:T(8,128)S(1)} %fusion.74), kind=kOutput, calls=%fused_computation.4.clone.1 | convolution fusion | flops 1611661312 | bytes 6553600 | tf_op jit(solution)/shard_map/while/body/eval_jaxpr/pij,pjk->pik/dot_general | solution.py:12
  172.3 3.6 %fusion.76 = f32[8,256,256]{2,1,0:T(8,128)} fusion(f32[8,256,256]{2,1,0:T(8,128)S(1)} %copy.104, f32[8,256,256]{2,1,0:T(8,128)S(1)} %fusion.73, f32[256,256]{1,0:T(8,128)S(1)} %fusion.74), kind=kOutput, calls=%fused_computation.2.clone.1 | convolution fusion | flops 1611661312 | bytes 6553600 | tf_op jit(solution)/shard_map/while/body/eval_jaxpr/pij,pjk->pik/dot_general | solution.py:12
  178.3 2.2 fusion.73
  180.5 4.9 %fusion.75 = f32[8,256,256]{1,2,0:T(8,128)} fusion(f32[8,256,256]{1,2,0:T(8,128)S(1)} %copy.103, f32[8,256,256]{2,1,0:T(8,128)S(1)} %fusion.73, f32[256,256]{1,0:T(8,128)S(1)} %fusion.74), kind=kOutput, calls=%fused_computation.4.clone.1 | convolution fusion | flops 1611661312 | bytes 6553600 | tf_op jit(solution)/shard_map/while/body/eval_jaxpr/pij,pjk->pik/dot_general | solution.py:12
  185.4 3.6 %fusion.76 = f32[8,256,256]{2,1,0:T(8,128)} fusion(f32[8,256,256]{2,1,0:T(8,128)S(1)} %copy.104, f32[8,256,256]{2,1,0:T(8,128)S(1)} %fusion.73, f32[256,256]{1,0:T(8,128)S(1)} %fusion.74), kind=kOutput, calls=%fused_computation.2.clone.1 | convolution fusion | flops 1611661312 | bytes 6553600 | tf_op jit(solution)/shard_map/while/body/eval_jaxpr/pij,pjk->pik/dot_general | solution.py:12
  191.4 2.2 fusion.73
  193.6 4.9 %fusion.75 = f32[8,256,256]{1,2,0:T(8,128)} fusion(f32[8,256,256]{1,2,0:T(8,128)S(1)} %copy.103, f32[8,256,256]{2,1,0:T(8,128)S(1)} %fusion.73, f32[256,256]{1,0:T(8,128)S(1)} %fusion.74), kind=kOutput, calls=%fused_computation.4.clone.1 | convolution fusion | flops 1611661312 | bytes 6553600 | tf_op jit(solution)/shard_map/while/body/eval_jaxpr/pij,pjk->pik/dot_general | solution.py:12
  198.5 3.6 %fusion.76 = f32[8,256,256]{2,1,0:T(8,128)} fusion(f32[8,256,256]{2,1,0:T(8,128)S(1)} %copy.104, f32[8,256,256]{2,1,0:T(8,128)S(1)} %fusion.73, f32[256,256]{1,0:T(8,128)S(1)} %fusion.74), kind=kOutput, calls=%fused_computation.2.clone.1 | convolution fusion | flops 1611661312 | bytes 6553600 | tf_op jit(solution)/shard_map/while/body/eval_jaxpr/pij,pjk->pik/dot_general | solution.py:12
  204.5 2.2 fusion.73
  206.7 4.9 %fusion.75 = f32[8,256,256]{1,2,0:T(8,128)} fusion(f32[8,256,256]{1,2,0:T(8,128)S(1)} %copy.103, f32[8,256,256]{2,1,0:T(8,128)S(1)} %fusion.73, f32[256,256]{1,0:T(8,128)S(1)} %fusion.74), kind=kOutput, calls=%fused_computation.4.clone.1 | convolution fusion | flops 1611661312 | bytes 6553600 | tf_op jit(solution)/shard_map/while/body/eval_jaxpr/pij,pjk->pik/dot_general | solution.py:12
  211.7 3.6 %fusion.76 = f32[8,256,256]{2,1,0:T(8,128)} fusion(f32[8,256,256]{2,1,0:T(8,128)S(1)} %copy.104, f32[8,256,256]{2,1,0:T(8,128)S(1)} %fusion.73, f32[256,256]{1,0:T(8,128)S(1)} %fusion.74), kind=kOutput, calls=%fused_computation.2.clone.1 | convolution fusion | flops 1611661312 | bytes 6553600 | tf_op jit(solution)/shard_map/while/body/eval_jaxpr/pij,pjk->pik/dot_general | solution.py:12
  217.7 2.2 fusion.73
  219.9 4.9 %fusion.75 = f32[8,256,256]{1,2,0:T(8,128)} fusion(f32[8,256,256]{1,2,0:T(8,128)S(1)} %copy.103, f32[8,256,256]{2,1,0:T(8,128)S(1)} %fusion.73, f32[256,256]{1,0:T(8,128)S(1)} %fusion.74), kind=kOutput, calls=%fused_computation.4.clone.1 | convolution fusion | flops 1611661312 | bytes 6553600 | tf_op jit(solution)/shard_map/while/body/eval_jaxpr/pij,pjk->pik/dot_general | solution.py:12
  224.8 3.6 %fusion.76 = f32[8,256,256]{2,1,0:T(8,128)} fusion(f32[8,256,256]{2,1,0:T(8,128)S(1)} %copy.104, f32[8,256,256]{2,1,0:T(8,128)S(1)} %fusion.73, f32[256,256]{1,0:T(8,128)S(1)} %fusion.74), kind=kOutput, calls=%fused_computation.2.clone.1 | convolution fusion | flops 1611661312 | bytes 6553600 | tf_op jit(solution)/shard_map/while/body/eval_jaxpr/pij,pjk->pik/dot_general | solution.py:12
  230.8 2.2 fusion.73
  233.0 4.9 %fusion.75 = f32[8,256,256]{1,2,0:T(8,128)} fusion(f32[8,256,256]{1,2,0:T(8,128)S(1)} %copy.103, f32[8,256,256]{2,1,0:T(8,128)S(1)} %fusion.73, f32[256,256]{1,0:T(8,128)S(1)} %fusion.74), kind=kOutput, calls=%fused_computation.4.clone.1 | convolution fusion | flops 1611661312 | bytes 6553600 | tf_op jit(solution)/shard_map/while/body/eval_jaxpr/pij,pjk->pik/dot_general | solution.py:12
  237.9 3.6 %fusion.76 = f32[8,256,256]{2,1,0:T(8,128)} fusion(f32[8,256,256]{2,1,0:T(8,128)S(1)} %copy.104, f32[8,256,256]{2,1,0:T(8,128)S(1)} %fusion.73, f32[256,256]{1,0:T(8,128)S(1)} %fusion.74), kind=kOutput, calls=%fused_computation.2.clone.1 | convolution fusion | flops 1611661312 | bytes 6553600 | tf_op jit(solution)/shard_map/while/body/eval_jaxpr/pij,pjk->pik/dot_general | solution.py:12
  241.4 1.7 copy.103
  243.9 2.2 fusion.73
  246.1 4.9 %fusion.75 = f32[8,256,256]{1,2,0:T(8,128)} fusion(f32[8,256,256]{1,2,0:T(8,128)S(1)} %copy.103, f32[8,256,256]{2,1,0:T(8,128)S(1)} %fusion.73, f32[256,256]{1,0:T(8,128)S(1)} %fusion.74), kind=kOutput, calls=%fused_computation.4.clone.1 | convolution fusion | flops 1611661312 | bytes 6553600 | tf_op jit(solution)/shard_map/while/body/eval_jaxpr/pij,pjk->pik/dot_general | solution.py:12
  251.0 3.6 %fusion.76 = f32[8,256,256]{2,1,0:T(8,128)} fusion(f32[8,256,256]{2,1,0:T(8,128)S(1)} %copy.104, f32[8,256,256]{2,1,0:T(8,128)S(1)} %fusion.73, f32[256,256]{1,0:T(8,128)S(1)} %fusion.74), kind=kOutput, calls=%fused_computation.2.clone.1 | convolution fusion | flops 1611661312 | bytes 6553600 | tf_op jit(solution)/shard_map/while/body/eval_jaxpr/pij,pjk->pik/dot_general | solution.py:12
  254.5 3.7 %fusion.49 = f32[8,1,256]{2,1,0:T(1,128)S(1)} fusion(f32[8,256,1]{1,0,2:T(8,128)S(1)} %bitcast.90, f32[8,256,256]{2,1,0:T(8,128)} %get-tuple-element.24, f32[8]{0:T(128)S(1)} %sqrt.7), kind=kOutput, calls=%fused_computation.63 | convolution fusion | flops 6815744 | bytes 2113568 | tf_op jit(solution)/shard_map/pij,pj->pi/dot_general | solution.py:68
  258.3 2.0 fusion.47
  260.3 5.9 %add_bitcast_fusion = f32[256,8,256]{0,2,1:T(8,128)} fusion(f32[256,8,256]{2,1,0:T(8,128)S(1)} %copy-done.4, f32[8,256]{1,0:T(8,128)S(1)} %bitcast.91, f32[8,256]{1,0:T(8,128)S(1)} %broadcast_multiply_fusion.1, f32[8,256,256]{2,1,0:T(8,128)S(1)} %copy-done.2, f32[8]{0:T(128)S(1)} %sqrt.7), kind=kOutput, calls=%fused_computation.28 | convolution fusion | flops 1612709888 | bytes 6307872 | tf_op jit(solution)/shard_map/pjk,jpc->kpc/dot_general | solution.py:73
  266.2 3.1 copy.48
  269.2 5.8 %all-to-all-start.1 = ((f32[256,8,256]{2,1,0:T(8,128)}), f32[256,8,256]{2,1,0:T(8,128)}, u32[]{:S(2)}, u32[]{:S(2)}) async-start(f32[256,8,256]{2,1,0:T(8,128)} %copy.48), calls=%async_computation.1 | async-start | bytes 4194304 | tf_op jit(solution)/shard_map/all_to_all | solution.py:74
  275.0 3.2 multiply_bitcast_fusion
  278.3 43.1 %all-to-all-done.1 = f32[256,8,256]{2,1,0:T(8,128)} async-done(((f32[256,8,256]{2,1,0:T(8,128)}), f32[256,8,256]{2,1,0:T(8,128)}, u32[]{:S(2)}, u32[]{:S(2)}) %all-to-all-start.1) | async-done | bytes 2097184 | tf_op jit(solution)/shard_map/all_to_all | solution.py:74
  321.4 4.1 %fusion.32 = f32[32,64,256]{2,1,0:T(8,128)} fusion(f32[32,8,8,256]{3,2,0,1:T(8,128)} %bitcast.24, s32[64]{0:T(128)S(1)} %bitcast.96), kind=kOutput, calls=%fused_computation.38 | convolution fusion | flops 402657280 | bytes 4194560 | tf_op jit(solution)/shard_map/kjc,qj->kqc/dot_general | solution.py:75
  (86 shorter events, 26.5 us)
Async XLA Ops:
  0.6 1.6 copy-start
  6.7 7.0 %copy-start.6 = (f32[1,8,512]{2,1,0:T(8,128)S(1)}, f32[1,8,512]{2,1,0:T(8,128)}, u32[]{:S(2)}) copy-start(f32[1,8,512]{2,1,0:T(8,128)} %param.15) | copy-start | bytes 49156
  6.7 7.0 %copy-start.8 = (s32[1,8]{1,0:T(1,128)S(1)}, s32[1,8]{1,0:T(1,128)}, u32[]{:S(2)}) copy-start(s32[1,8]{1,0:T(1,128)} %param.13) | copy-start | bytes 100
  6.7 53.0 %all-to-all-start = ((f32[32,64,256]{2,0,1:T(8,128)}), f32[32,64,256]{2,0,1:T(8,128)}, u32[]{:S(2)}, u32[]{:S(2)}) async-start(f32[32,64,256]{2,0,1:T(8,128)} %copy.41), calls=%async_computation | async-start | bytes 4194304 | tf_op jit(solution)/shard_map/all_to_all | solution.py:42
  69.1 3.2 copy-start.3
  69.1 3.2 copy-start.5
  78.3 4.3 %copy-start.7 = (f32[1,8,512]{2,1,0:T(8,128)S(1)}, f32[1,8,512]{2,1,0:T(8,128)}, u32[]{:S(2)}) copy-start(f32[1,8,512]{2,1,0:T(8,128)} %param.14) | copy-start | bytes 49156
  97.2 2.2 copy-start.1
  110.3 2.2 copy-start.1
  123.4 2.2 copy-start.1
  136.5 2.2 copy-start.1
  149.7 2.2 copy-start.1
  162.8 2.2 copy-start.1
  175.9 2.2 copy-start.1
  189.0 2.2 copy-start.1
  202.1 2.2 copy-start.1
  215.2 2.2 copy-start.1
  228.3 2.2 copy-start.1
  241.4 2.2 copy-start.1
  254.5 3.7 %copy-start.2 = (f32[8,256,256]{2,1,0:T(8,128)S(1)}, f32[8,256,256]{2,1,0:T(8,128)}, u32[]{:S(2)}) copy-start(f32[8,256,256]{2,1,0:T(8,128)} %get-tuple-element.24) | copy-start | bytes 6291460
  258.3 2.0 copy-start.4
  269.2 52.2 %all-to-all-start.1 = ((f32[256,8,256]{2,1,0:T(8,128)}), f32[256,8,256]{2,1,0:T(8,128)}, u32[]{:S(2)}, u32[]{:S(2)}) async-start(f32[256,8,256]{2,1,0:T(8,128)} %copy.48), calls=%async_computation.1 | async-start | bytes 4194304 | tf_op jit(solution)/shard_map/all_to_all | solution.py:74
  275.0 46.4 %copy-start.9 = (s32[1,64]{1,0:T(1,128)S(1)}, s32[1,64]{1,0:T(1,128)}, u32[]{:S(2)}) copy-start(s32[1,64]{1,0:T(1,128)} %param.11) | copy-start | bytes 772
where the time goes:
time: 329 us; the launch traced here: 326 us
  matrix products  161 us (49%)
  waiting for transfers between devices  89 us (27%)
  local copies, waits for them, and re-layouts  51.3 us (16%)
  starting transfers between devices  12 us (4%)
  other arithmetic  11.2 us (3%)
    dot_general x36, matrix products, batched(): jnp.einsum('pij,pjk->pik', left, right, precision=lax.Precision.HIGHEST)  128 us
    all_to_all x1, waiting for transfers between devices, local(): lax.all_to_all(listed, 'mem', split_axis=1, concat_axis=0, tiled=True)  45.9 us
    all_to_all x1, waiting for transfers between devices, local(): lax.all_to_all(updated, 'mem', split_axis=0, concat_axis=1, tiled=True)  43.1 us
    while x48, local copies, waits for them, and re-layouts  29.3 us
  transfers between devices with their start and end apart: 2, of which 2 were waited for; matrix products, arithmetic and copies ran while one was open for 1% of the time, Pallas kernels for 0%

commit v1 on v0

v1 whole, which is shorter than its diff:
```python
import functools
import math

import jax
import jax.numpy as jnp
from jax import lax
from jax.experimental import pallas as pl
from jax.experimental.pallas import tpu as pltpu
from jax.sharding import PartitionSpec as P

ITERS = 12
LIGHT = 6
CHUNKS = 4
HIGHEST = lax.Precision.HIGHEST


def whole():
    return pl.BlockSpec(memory_space=pltpu.VMEM)


def pieces(x):
    high = x.astype(jnp.bfloat16)
    return high, (x - high.astype(jnp.float32)).astype(jnp.bfloat16)


def product(left, right, full):
    lh, ll = left
    rh, rl = right
    lefts = [lh, lh, ll, ll] if full else [lh, lh, ll]
    rights = [rh, rl, rh, rl] if full else [rh, rl, rh]
    return jnp.dot(
        jnp.concatenate(lefts, axis=1),
        jnp.concatenate(rights, axis=0),
        preferred_element_type=jnp.float32,
    )


def exact(left, right, right_dim=0):
    return lax.dot_general(
        left, right, (((1,), (right_dim,)), ((), ())),
        precision=HIGHEST, preferred_element_type=jnp.float32,
    )


def sweep(y_ref, z_ref, group, full, last):
    for g in range(group):
        y, z = y_ref[g], z_ref[g]
        yp, zp = pieces(y), pieces(z)
        turn = pieces(product(zp, yp, full))
        if not last:
            y_ref[g] = 1.5 * y - 0.5 * product(yp, turn, full)
        z_ref[g] = 1.5 * z - 0.5 * product(turn, zp, full)


def analyse(group, per_worker, first, worker_ref, count_ref, state_ref, op_ref, index_ref, value_ref, weight_ref, *rest):
    spread_ref, out_ref, pert_ref, y_ref, z_ref, row_ref = rest[-6:]
    workers, _, rows_dev, cells = state_ref.shape
    members = workers * rows_dev
    levels = op_ref.shape[0]
    slots = index_ref.shape[1]
    step = pl.program_id(0)
    worker = worker_ref[0]
    eye = (
        lax.broadcasted_iota(jnp.int32, (members, members), 0)
        == lax.broadcasted_iota(jnp.int32, (members, members), 1)
    )
    scales = []
    for g in range(group):
        spot = first + step * group + g
        state = state_ref[:, g].reshape(members, cells)
        mean = jnp.mean(state, axis=0, keepdims=True)
        pert = state - mean
        pert_ref[g] = pert
        op = op_ref[...]
        columns = cells // levels
        chan = jnp.concatenate([exact(pert[:, c * levels:(c + 1) * levels], op) for c in range(columns)], axis=1)
        wide = jnp.broadcast_to(mean, (8, cells))
        chan_mean = jnp.concatenate([exact(wide[:, c * levels:(c + 1) * levels], op) for c in range(columns)], axis=1)
        width = chan.shape[1]
        index = index_ref[pl.ds(worker * per_worker + spot, 1), :]
        live = lax.broadcasted_iota(jnp.int32, (1, slots), 1) < count_ref[spot]
        weight = jnp.where(live, weight_ref[pl.ds(spot, 1), :], 0.0)
        value = weight * value_ref[pl.ds(spot, 1), :]
        picker = (lax.broadcasted_iota(jnp.int32, (width, slots), 0) == index).astype(jnp.bfloat16)
        sub = lax.broadcasted_iota(jnp.int32, (16, slots), 0)
        stack = jnp.where(sub == 0, weight, jnp.where(sub == 1, value, 0.0))
        s0 = stack.astype(jnp.bfloat16)
        left = stack - s0.astype(jnp.float32)
        s1 = left.astype(jnp.bfloat16)
        s2 = (left - s1.astype(jnp.float32)).astype(jnp.bfloat16)
        binned = sum(
            lax.dot_general(s, picker, (((1,), (1,)), ((), ())), preferred_element_type=jnp.float32)
            for s in (s2, s1, s0)
        )
        total = binned[0:1]
        innov = binned[1:2] - chan_mean[0:1] * total
        system = exact(chan * total, chan, 1) + jnp.where(eye, members - 1.0, 0.0)
        row_ref[g] = exact(jnp.broadcast_to(innov, (8, width)), chan, 1)
        trace_value = jnp.sum(jnp.sum(jnp.where(eye, system, 0.0), axis=0, keepdims=True), axis=1, keepdims=True)
        y = system / trace_value
        scales.append(trace_value)
        yp = pieces(y)
        z_ref[g] = jnp.where(eye, 1.5, 0.0) - 0.5 * y
        y_ref[g] = 1.5 * y - 0.5 * product(yp, yp, False)

    def light(k, carry):
        sweep(y_ref, z_ref, group, False, False)
        return carry

    def firm(k, carry):
        sweep(y_ref, z_ref, group, True, False)
        return carry

    lax.fori_loop(1, LIGHT, light, 0)
    lax.fori_loop(LIGHT, ITERS - 1, firm, 0)
    sweep(y_ref, z_ref, group, True, True)

    for g in range(group):
        z = z_ref[g]
        trace_value = scales[g]
        spread = z * (math.sqrt(members - 1.0) / jnp.sqrt(trace_value))
        spread_ref[g] = spread
        weights = exact(exact(row_ref[g], z, 1), z, 1)[0:1] / trace_value
        state_mean = jnp.mean(state_ref[:, g].reshape(members, cells), axis=0, keepdims=True)
        coef = spread + weights
        update = state_mean + product(pieces(coef), pieces(pert_ref[g]), False)
        out_ref[:, g] = update.reshape(workers, rows_dev, cells)


def gather_kernel(n_mem, order_ref, x_ref, *rest):
    outs, lanes_ref = rest[:-1], rest[-1]
    halves, _, lanes = lanes_ref.shape
    for h in range(halves):
        lanes_ref[h] = x_ref[:, h * lanes:(h + 1) * lanes]
    band = order_ref.shape[0]
    per = outs[0].shape[1]
    rows = outs[0].shape[2]
    chunks = len(outs)
    for c, out in enumerate(outs):
        @pl.loop(0, n_mem * per)
        def _(t):
            w, i = t // per, lax.rem(t, per)
            q = order_ref[(w * chunks + c) * per + i]
            for h in range(halves):
                out[w, i, :, h * lanes:(h + 1) * lanes] = lanes_ref[h, pl.ds(q, rows, stride=band), :]


def scatter_kernel(n_mem, order_ref, *refs):
    ins, out, lanes_ref = refs[:-2], refs[-2], refs[-1]
    halves, _, lanes = lanes_ref.shape
    band = order_ref.shape[0]
    per = ins[0].shape[1]
    rows = ins[0].shape[2]
    chunks = len(ins)
    for c, block in enumerate(ins):
        @pl.loop(0, n_mem * per)
        def _(t):
            w, i = t // per, lax.rem(t, per)
            q = order_ref[(w * chunks + c) * per + i]
            for h in range(halves):
                lanes_ref[h, pl.ds(q, rows, stride=band), :] = block[w, i, :, h * lanes:(h + 1) * lanes]

    for h in range(halves):
        out[:, h * lanes:(h + 1) * lanes] = lanes_ref[h]


def local(ensemble, column_operator, patch_order, obs_index, obs_count, obs_values, obs_precision):
    rows_dev, band, cells = ensemble.shape
    slots = obs_index.shape[2]
    n_mem = lax.axis_size("mem")
    per_worker = band // n_mem
    members = rows_dev * n_mem
    chunks = CHUNKS if per_worker % CHUNKS == 0 else 1
    per = per_worker // chunks
    group = 2 if per % 2 == 0 else 1
    order = patch_order[0]
    worker = lax.axis_index("mem").astype(jnp.int32).reshape(1)
    smem = pl.BlockSpec(memory_space=pltpu.SMEM)
    block = jax.ShapeDtypeStruct((n_mem, per, rows_dev, cells), jnp.float32)

    sends = pl.pallas_call(
        functools.partial(gather_kernel, n_mem),
        out_shape=[block] * chunks,
        in_specs=[smem, whole()],
        out_specs=[whole()] * chunks,
        scratch_shapes=[pltpu.VMEM((cells // 128, rows_dev * band, 128), jnp.float32)],
        name="gather_patches",
    )(order, ensemble.reshape(rows_dev * band, cells))

    states = [lax.all_to_all(s, "mem", split_axis=0, concat_axis=0, tiled=True) for s in sends]

    spread_shape = jax.ShapeDtypeStruct((per_worker, members, members), jnp.float32)
    spread = None
    backs = []
    for c in range(chunks):
        first = c * per
        in_specs = [
            pl.BlockSpec((n_mem, group, rows_dev, cells), lambda i, *_: (0, i, 0, 0)),
            whole(), whole(), whole(), whole(),
        ]
        operands = [worker, obs_count[0], states[c], column_operator, obs_index[0], obs_values[0], obs_precision[0]]
        aliases = {}
        if spread is not None:
            in_specs.append(pl.BlockSpec(memory_space=pl.ANY))
            operands.append(spread)
            aliases = {7: 0}
        base = first // group
        spread, updated = pl.pallas_call(
            functools.partial(analyse, group, per_worker, first),
            out_shape=[spread_shape, block],
            grid_spec=pltpu.PrefetchScalarGridSpec(
                num_scalar_prefetch=2,
                grid=(per // group,),
                in_specs=in_specs,
                out_specs=[
                    pl.BlockSpec((group, members, members), lambda i, *_, base=base: (base + i, 0, 0)),
                    pl.BlockSpec((n_mem, group, rows_dev, cells), lambda i, *_: (0, i, 0, 0)),
                ],
                scratch_shapes=[
                    pltpu.VMEM((group, members, cells), jnp.float32),
                    pltpu.VMEM((group, members, members), jnp.float32),
                    pltpu.VMEM((group, members, members), jnp.float32),
                    pltpu.VMEM((group, 8, members), jnp.float32),
                ],
            ),
            input_output_aliases=aliases,
            cost_estimate=pl.CostEstimate(
                flops=per * 36 * 4 * 2 * members ** 3, transcendentals=0,
                bytes_accessed=per * 4 * (2 * members * cells + members * members),
            ),
            name=f"analyse_{c}",
        )(*operands)
        backs.append(lax.all_to_all(updated, "mem", split_axis=0, concat_axis=0, tiled=True))

    restored = pl.pallas_call(
        functools.partial(scatter_kernel, n_mem),
        out_shape=jax.ShapeDtypeStruct((rows_dev * band, cells), jnp.float32),
        in_specs=[smem] + [whole()] * chunks,
        out_specs=whole(),
        scratch_shapes=[pltpu.VMEM((cells // 128, rows_dev * band, 128), jnp.float32)],
        name="restore_patches",
    )(order, *backs)
    return (restored.reshape(rows_dev, band, cells), spread[None])


def solution(mesh):
    placed = (
        P("mem", "band", None),
        P(),
        P("band", None),
        P("band", None, None),
        P("band", "mem"),
        P("band", "mem", None),
        P("band", "mem", None),
    )
    return jax.shard_map(
        local,
        mesh=mesh,
        in_specs=placed,
        out_specs=(P("mem", "band", None), P("band", "mem", None, None)),
        check_vma=False,
    )
```

time: 329 us -> 198 us (0.60)
  the two profiles are of different devices: /device:TPU:24 before, /device:TPU:0 now
where the time goes in v1:
time: 198 us; the launch traced here: 197 us
  Pallas kernels  99.6 us (50%)
  blocking collectives  75.4 us (38%)
  starting transfers between devices  21.7 us (11%)
    pallas_call x4, Pallas kernels, local(): pl.pallas_call(functools.partial(analyse, group, per_worker, first), out_...  88.2 us
    all_to_all x3, blocking collectives, local(): lax.all_to_all(s, 'mem', split_axis=0, concat_axis=0, tiled=True)  57.5 us
    all_to_all x3, starting transfers between devices, local(): lax.all_to_all(updated, 'mem', split_axis=0, concat_axis=0, tiled=True)  18 us
    all_to_all x1, blocking collectives, local(): lax.all_to_all(updated, 'mem', split_axis=0, concat_axis=0, tiled=True)  17.9 us
    pallas_call x1, Pallas kernels, local(): pl.pallas_call(functools.partial(gather_kernel, n_mem), out_shape=[block]...  6.11 us
    pallas_call x1, Pallas kernels, local(): pl.pallas_call(functools.partial(scatter_kernel, n_mem), out_shape=jax.Sh...  5.23 us
  transfers between devices with their start and end apart: 4, of which 0 were waited for; matrix products, arithmetic and copies ran while one was open for 0% of the time, Pallas kernels for 45%

profile of v1, /device:TPU:0, one launch (start us, length us, event | category | flops | bytes accessed | tf_op | source)
XLA Modules:
  0.0 197.4 jit_solution(14532968533419568338)
XLA Ops:
  0.6 6.1 %gather_patches.1 = (f32[8,2,32,256]{3,2,1,0:T(8,128)}, f32[8,2,32,256]{3,2,1,0:T(8,128)}, f32[8,2,32,256]{3,2,1,0:T(8,128)}, f32[8,2,32,256]{3,2,1,0:T(8,128)}) custom-call(s32[64]{0:T(128)} %bitcast.11, f32[2048,256]{1,0:T(8,128)} %bitcast.9), custom_call_target="tpu_custom_call" | custom-call | tf_op jit(solution)/shard_map/gather_patches/pallas_call | solution.py:181
  6.7 0.0 copy-start.4
  6.7 22.1 %all_to_all.40.state_ref = f32[8,2,32,256]{3,2,1,0:T(8,128)} all-to-all(f32[8,2,32,256]{3,2,1,0:T(8,128)} %get-tuple-element.14), channel_id=1, replica_groups=mesh['mem'=8,'band'=4] {'mem'}, dimensions={0} | all-to-all | bytes 1048576 | tf_op jit(solution)/shard_map/all_to_all | solution.py:190
  28.8 17.8 %all_to_all.41.state_ref = f32[8,2,32,256]{3,2,1,0:T(8,128)} all-to-all(f32[8,2,32,256]{3,2,1,0:T(8,128)} %get-tuple-element.16), channel_id=1, replica_groups=mesh['mem'=8,'band'=4] {'mem'}, dimensions={0} | all-to-all | bytes 1048576 | tf_op jit(solution)/shard_map/all_to_all | solution.py:190
  46.6 0.0 copy-done.4
  46.6 17.6 %all_to_all.42.state_ref = f32[8,2,32,256]{3,2,1,0:T(8,128)} all-to-all(f32[8,2,32,256]{3,2,1,0:T(8,128)S(1)} %copy-done.4), channel_id=1, replica_groups=mesh['mem'=8,'band'=4] {'mem'}, dimensions={0} | all-to-all | bytes 1048576 | tf_op jit(solution)/shard_map/all_to_all | solution.py:190
  64.2 3.6 %all-to-all-start.6 = ((f32[8,2,32,256]{3,2,1,0:T(8,128)}), f32[8,2,32,256]{3,2,1,0:T(8,128)S(1)}, u32[]{:S(2)}, u32[]{:S(2)}) async-start(f32[8,2,32,256]{3,2,1,0:T(8,128)} %get-tuple-element.22), calls=%async_computation.6 | async-start | bytes 1048576 | tf_op jit(solution)/shard_map/all_to_all | solution.py:190
  67.9 22.0 %analyse_0.1 = (f32[8,256,256]{2,1,0:T(8,128)}, f32[8,2,32,256]{3,2,1,0:T(8,128)}) custom-call(s32[1]{0:T(128)} %bitcast.1.worker_ref, s32[8]{0:T(128)} %bitcast.25, f32[8,2,32,256]{3,2,1,0:T(8,128)} %all_to_all.40.state_ref, f32[128,128]{1,0:T(8,128)} %op_ref.7, s32[64,512]{1,0:T(8,128)} %bitcast.13, f32[8,512]{1,0:T(8,128)} %bitcast.17, f32[8,512]{1,0:T(8,128)} %bitcast.21), custom_call_target="tpu_custom_call" | custom-call | flops 9663676416 | bytes 1572864 | tf_op jit(solution)/shard_map/analyse_0/pallas_call | solution.py:208
  89.9 0.0 all-to-all-done.6.state_ref
  89.9 0.0 copy-start.3
  89.9 6.0 %all-to-all-start.1 = ((f32[8,2,32,256]{3,2,1,0:T(8,128)}), f32[8,2,32,256]{3,2,1,0:T(8,128)S(1)}, u32[]{:S(2)}, u32[]{:S(2)}) async-start(f32[8,2,32,256]{3,2,1,0:T(8,128)} %get-tuple-element.15), calls=%async_computation.1 | async-start | bytes 1048576 | tf_op jit(solution)/shard_map/all_to_all | solution.py:233
  95.9 22.1 %analyse_1.1 = (f32[8,256,256]{2,1,0:T(8,128)}, f32[8,2,32,256]{3,2,1,0:T(8,128)}) custom-call(s32[1]{0:T(128)} %bitcast.1.worker_ref, s32[8]{0:T(128)} %bitcast.26, f32[8,2,32,256]{3,2,1,0:T(8,128)} %all_to_all.41.state_ref, f32[128,128]{1,0:T(8,128)} %op_ref.7, s32[64,512]{1,0:T(8,128)} %bitcast.14, ...), custom_call_target="tpu_custom_call", output_to_operand_aliasing={{0}: (7, {})} | custom-call | flops 9663676416 | bytes 1572864 | tf_op jit(solution)/shard_map/analyse_1/pallas_call | solution.py:208
  118.0 0.0 copy-done.3
  118.0 0.0 all-to-all-done.1.refs_0_
  118.0 0.0 copy-start
  118.0 6.0 %all-to-all-start.3 = ((f32[8,2,32,256]{3,2,1,0:T(8,128)}), f32[8,2,32,256]{3,2,1,0:T(8,128)S(1)}, u32[]{:S(2)}, u32[]{:S(2)}) async-start(f32[8,2,32,256]{3,2,1,0:T(8,128)} %get-tuple-element.18), calls=%async_computation.3 | async-start | bytes 1048576 | tf_op jit(solution)/shard_map/all_to_all | solution.py:233
  124.0 22.1 %analyse_2.1 = (f32[8,256,256]{2,1,0:T(8,128)}, f32[8,2,32,256]{3,2,1,0:T(8,128)}) custom-call(s32[1]{0:T(128)} %bitcast.1.worker_ref, s32[8]{0:T(128)} %bitcast.27, f32[8,2,32,256]{3,2,1,0:T(8,128)} %all_to_all.42.state_ref, f32[128,128]{1,0:T(8,128)} %op_ref.7, s32[64,512]{1,0:T(8,128)} %bitcast.15, ...), custom_call_target="tpu_custom_call", output_to_operand_aliasing={{0}: (7, {})} | custom-call | flops 9663676416 | bytes 1572864 | tf_op jit(solution)/shard_map/analyse_2/pallas_call | solution.py:208
  146.1 0.0 copy-done
  146.1 0.0 all-to-all-done.3.refs_1_
  146.1 0.0 copy-start.1
  146.1 6.0 %all-to-all-start.5 = ((f32[8,2,32,256]{3,2,1,0:T(8,128)}), f32[8,2,32,256]{3,2,1,0:T(8,128)S(1)}, u32[]{:S(2)}, u32[]{:S(2)}) async-start(f32[8,2,32,256]{3,2,1,0:T(8,128)} %get-tuple-element.21), calls=%async_computation.5 | async-start | bytes 1048576 | tf_op jit(solution)/shard_map/all_to_all | solution.py:233
  152.1 22.1 %analyse_3.1 = (f32[8,256,256]{2,1,0:T(8,128)}, f32[8,2,32,256]{3,2,1,0:T(8,128)}) custom-call(s32[1]{0:T(128)} %bitcast.1.worker_ref, s32[8]{0:T(128)} %bitcast.28, f32[8,2,32,256]{3,2,1,0:T(8,128)} %copy-done.3, f32[128,128]{1,0:T(8,128)} %op_ref.7, s32[64,512]{1,0:T(8,128)} %bitcast.16, f32[8,512]{1,0:T(8,128)} %bitcast.20, ...), custom_call_target="tpu_custom_call", output_to_operand_aliasing={{0}: (7, {})} | custom-call | flops 9663676416 | bytes 1572864 | tf_op jit(solution)/shard_map/analyse_3/pallas_call | solution.py:208
  174.2 0.0 copy-done.1
  174.2 0.0 all-to-all-done.5.refs_2_
  174.2 0.0 copy-start.2
  174.2 17.9 %all_to_all.43.refs_3_ = f32[8,2,32,256]{3,2,1,0:T(8,128)} all-to-all(f32[8,2,32,256]{3,2,1,0:T(8,128)} %get-tuple-element.24), channel_id=1, replica_groups=mesh['mem'=8,'band'=4] {'mem'}, dimensions={0} | all-to-all | bytes 1048576 | tf_op jit(solution)/shard_map/all_to_all | solution.py:233
  192.1 0.0 copy-done.2
  192.1 5.2 %restore_patches.1 = f32[2048,256]{1,0:T(8,128)} custom-call(s32[64]{0:T(128)} %bitcast.12, f32[8,2,32,256]{3,2,1,0:T(8,128)} %copy-done, f32[8,2,32,256]{3,2,1,0:T(8,128)} %copy-done.1, f32[8,2,32,256]{3,2,1,0:T(8,128)} %copy-done.2, f32[8,2,32,256]{3,2,1,0:T(8,128)} %all_to_all.43.refs_3_), custom_call_target="tpu_custom_call" | custom-call | tf_op jit(solution)/shard_map/restore_patches/pallas_call | solution.py:235
Async XLA Ops:
  6.7 39.9 %copy-start.4 = (f32[8,2,32,256]{3,2,1,0:T(8,128)S(1)}, f32[8,2,32,256]{3,2,1,0:T(8,128)}, u32[]{:S(2)}) copy-start(f32[8,2,32,256]{3,2,1,0:T(8,128)} %get-tuple-element.19) | copy-start | bytes 1572868
  64.2 25.7 %all-to-all-start.6 = ((f32[8,2,32,256]{3,2,1,0:T(8,128)}), f32[8,2,32,256]{3,2,1,0:T(8,128)S(1)}, u32[]{:S(2)}, u32[]{:S(2)}) async-start(f32[8,2,32,256]{3,2,1,0:T(8,128)} %get-tuple-element.22), calls=%async_computation.6 | async-start | bytes 1048576 | tf_op jit(solution)/shard_map/all_to_all | solution.py:190
  89.9 28.1 %copy-start.3 = (f32[8,2,32,256]{3,2,1,0:T(8,128)}, f32[8,2,32,256]{3,2,1,0:T(8,128)S(1)}, u32[]{:S(2)}) copy-start(f32[8,2,32,256]{3,2,1,0:T(8,128)S(1)} %all-to-all-done.6.state_ref) | copy-start | bytes 1572868
  89.9 28.1 %all-to-all-start.1 = ((f32[8,2,32,256]{3,2,1,0:T(8,128)}), f32[8,2,32,256]{3,2,1,0:T(8,128)S(1)}, u32[]{:S(2)}, u32[]{:S(2)}) async-start(f32[8,2,32,256]{3,2,1,0:T(8,128)} %get-tuple-element.15), calls=%async_computation.1 | async-start | bytes 1048576 | tf_op jit(solution)/shard_map/all_to_all | solution.py:233
  118.0 28.1 %copy-start = (f32[8,2,32,256]{3,2,1,0:T(8,128)}, f32[8,2,32,256]{3,2,1,0:T(8,128)S(1)}, u32[]{:S(2)}) copy-start(f32[8,2,32,256]{3,2,1,0:T(8,128)S(1)} %all-to-all-done.1.refs_0_) | copy-start | bytes 1572868
  118.0 28.1 %all-to-all-start.3 = ((f32[8,2,32,256]{3,2,1,0:T(8,128)}), f32[8,2,32,256]{3,2,1,0:T(8,128)S(1)}, u32[]{:S(2)}, u32[]{:S(2)}) async-start(f32[8,2,32,256]{3,2,1,0:T(8,128)} %get-tuple-element.18), calls=%async_computation.3 | async-start | bytes 1048576 | tf_op jit(solution)/shard_map/all_to_all | solution.py:233
  146.1 28.1 %copy-start.1 = (f32[8,2,32,256]{3,2,1,0:T(8,128)}, f32[8,2,32,256]{3,2,1,0:T(8,128)S(1)}, u32[]{:S(2)}) copy-start(f32[8,2,32,256]{3,2,1,0:T(8,128)S(1)} %all-to-all-done.3.refs_1_) | copy-start | bytes 1572868
  146.1 28.1 %all-to-all-start.5 = ((f32[8,2,32,256]{3,2,1,0:T(8,128)}), f32[8,2,32,256]{3,2,1,0:T(8,128)S(1)}, u32[]{:S(2)}, u32[]{:S(2)}) async-start(f32[8,2,32,256]{3,2,1,0:T(8,128)} %get-tuple-element.21), calls=%async_computation.5 | async-start | bytes 1048576 | tf_op jit(solution)/shard_map/all_to_all | solution.py:233
  174.2 17.9 %copy-start.2 = (f32[8,2,32,256]{3,2,1,0:T(8,128)}, f32[8,2,32,256]{3,2,1,0:T(8,128)S(1)}, u32[]{:S(2)}) copy-start(f32[8,2,32,256]{3,2,1,0:T(8,128)S(1)} %all-to-all-done.5.refs_2_) | copy-start | bytes 1572868

commit v2 on v1

--- a/solution.py
+++ b/solution.py
@@ -10,7 +10,7 @@
 
 ITERS = 12
 LIGHT = 6
-CHUNKS = 4
+MESH = pl.DeviceIdType.MESH
 HIGHEST = lax.Precision.HIGHEST
 
 
@@ -52,22 +52,82 @@
         z_ref[g] = 1.5 * z - 0.5 * product(turn, zp, full)
 
 
-def analyse(group, per_worker, first, worker_ref, count_ref, state_ref, op_ref, index_ref, value_ref, weight_ref, *rest):
-    spread_ref, out_ref, pert_ref, y_ref, z_ref, row_ref = rest[-6:]
-    workers, _, rows_dev, cells = state_ref.shape
+def analyse(n_mem, group, count_ref, sends_ref, op_ref, index_ref, value_ref, weight_ref, spread_ref, back_ref,
+            inbox, outbox, pert_ref, y_ref, z_ref, row_ref, in_send, in_recv, own_sem, out_send, out_recv, home_sem):
+    per_worker, workers, rows_dev, cells = inbox.shape
     members = workers * rows_dev
     levels = op_ref.shape[0]
     slots = index_ref.shape[1]
-    step = pl.program_id(0)
-    worker = worker_ref[0]
+    me = lax.axis_index("mem")
+
+    def greet(d, carry):
+        pl.semaphore_signal(barrier, inc=1, device_id={"mem": lax.rem(me + d, n_mem)}, device_id_type=MESH)
+        return carry
+
+    barrier = pltpu.get_barrier_semaphore()
+    lax.fori_loop(1, n_mem, greet, 0)
+    pl.semaphore_wait(barrier, n_mem - 1)
+
+    def own_in(i):
+        return pltpu.make_async_copy(sends_ref.at[me, i], inbox.at[i, me], own_sem.at[i])
+
+    def own_back(i):
+        return pltpu.make_async_copy(outbox.at[i, me], back_ref.at[me, i], home_sem.at[i])
+
+    def issue(i, carry):
+        own_in(i).start()
+
+        def one(d, carry):
+            peer = lax.rem(me + d, n_mem)
+            pltpu.make_async_remote_copy(
+                src_ref=sends_ref.at[peer, i], dst_ref=inbox.at[i, me],
+                send_sem=in_send, recv_sem=in_recv.at[i],
+                device_id={"mem": peer}, device_id_type=MESH,
+            ).start()
+            return carry
+
+        lax.fori_loop(1, n_mem, one, 0)
+        return carry
+
+    lax.fori_loop(0, per_worker, issue, 0)
     eye = (
         lax.broadcasted_iota(jnp.int32, (members, members), 0)
         == lax.broadcasted_iota(jnp.int32, (members, members), 1)
     )
-    scales = []
-    for g in range(group):
-        spot = first + step * group + g
-        state = state_ref[:, g].reshape(members, cells)
+
+    def step(t, carry):
+        for g in range(group):
+            spot = t * group + g
+            own_in(spot).wait()
+            arrived = inbox.at[spot, pl.ds(0, n_mem - 1)]
+            pltpu.make_async_copy(arrived, arrived, in_recv.at[spot]).wait()
+        scales = []
+        for g in range(group):
+            scales.append(prepare(t * group + g, g))
+        lax.fori_loop(1, LIGHT, light, 0)
+        lax.fori_loop(LIGHT, ITERS - 1, firm, 0)
+        sweep(y_ref, z_ref, group, True, True)
+        for g in range(group):
+            finish(t * group + g, g, scales[g])
+            launch(t * group + g)
+        return carry
+
+    def launch(spot):
+        own_back(spot).start()
+
+        def one(d, carry):
+            peer = lax.rem(me + d, n_mem)
+            pltpu.make_async_remote_copy(
+                src_ref=outbox.at[spot, peer], dst_ref=back_ref.at[me, spot],
+                send_sem=out_send, recv_sem=out_recv,
+                device_id={"mem": peer}, device_id_type=MESH,
+            ).start()
+            return carry
+
+        lax.fori_loop(1, n_mem, one, 0)
+
+    def prepare(spot, g):
+        state = inbox[spot].reshape(members, cells)
         mean = jnp.mean(state, axis=0, keepdims=True)
         pert = state - mean
         pert_ref[g] = pert
@@ -77,7 +137,7 @@
         wide = jnp.broadcast_to(mean, (8, cells))
         chan_mean = jnp.concatenate([exact(wide[:, c * levels:(c + 1) * levels], op) for c in range(columns)], axis=1)
         width = chan.shape[1]
-        index = index_ref[pl.ds(worker * per_worker + spot, 1), :]
+        index = index_ref[pl.ds(me * per_worker + spot, 1), :]
         live = lax.broadcasted_iota(jnp.int32, (1, slots), 1) < count_ref[spot]
         weight = jnp.where(live, weight_ref[pl.ds(spot, 1), :], 0.0)
         value = weight * value_ref[pl.ds(spot, 1), :]
@@ -98,10 +158,10 @@
         row_ref[g] = exact(jnp.broadcast_to(innov, (8, width)), chan, 1)
         trace_value = jnp.sum(jnp.sum(jnp.where(eye, system, 0.0), axis=0, keepdims=True), axis=1, keepdims=True)
         y = system / trace_value
-        scales.append(trace_value)
         yp = pieces(y)
         z_ref[g] = jnp.where(eye, 1.5, 0.0) - 0.5 * y
         y_ref[g] = 1.5 * y - 0.5 * product(yp, yp, False)
+        return trace_value
 
     def light(k, carry):
         sweep(y_ref, z_ref, group, False, False)
@@ -111,20 +171,24 @@
         sweep(y_ref, z_ref, group, True, False)
         return carry
 
-    lax.fori_loop(1, LIGHT, light, 0)
-    lax.fori_loop(LIGHT, ITERS - 1, firm, 0)
-    sweep(y_ref, z_ref, group, True, True)
-
-    for g in range(group):
+    def finish(spot, g, trace_value):
         z = z_ref[g]
-        trace_value = scales[g]
         spread = z * (math.sqrt(members - 1.0) / jnp.sqrt(trace_value))
-        spread_ref[g] = spread
+        spread_ref[spot] = spread
         weights = exact(exact(row_ref[g], z, 1), z, 1)[0:1] / trace_value
-        state_mean = jnp.mean(state_ref[:, g].reshape(members, cells), axis=0, keepdims=True)
+        state_mean = jnp.mean(inbox[spot].reshape(members, cells), axis=0, keepdims=True)
         coef = spread + weights
         update = state_mean + product(pieces(coef), pieces(pert_ref[g]), False)
-        out_ref[:, g] = update.reshape(workers, rows_dev, cells)
+        outbox[spot] = update.reshape(workers, rows_dev, cells)
+
+    lax.fori_loop(0, per_worker // group, step, 0)
+    sent = sends_ref.at[pl.ds(0, n_mem - 1)]
+    pltpu.make_async_copy(sent, sent, in_send).wait()
+    posted = back_ref.at[pl.ds(0, n_mem - 1)]
+    pltpu.make_async_copy(posted, posted, out_send).wait()
+    pltpu.make_async_copy(posted, posted, out_recv).wait()
+    for i in range(per_worker):
+        own_back(i).wait()
 
 
 def gather_kernel(n_mem, order_ref, x_ref, *rest):
@@ -170,76 +234,51 @@
     n_mem = lax.axis_size("mem")
     per_worker = band // n_mem
     members = rows_dev * n_mem
-    chunks = CHUNKS if per_worker % CHUNKS == 0 else 1
-    per = per_worker // chunks
-    group = 2 if per % 2 == 0 else 1
+    group = 2 if per_worker % 2 == 0 else 1
     order = patch_order[0]
-    worker = lax.axis_index("mem").astype(jnp.int32).reshape(1)
     smem = pl.BlockSpec(memory_space=pltpu.SMEM)
-    block = jax.ShapeDtypeStruct((n_mem, per, rows_dev, cells), jnp.float32)
-
-    sends = pl.pallas_call(
+    block = jax.ShapeDtypeStruct((n_mem, per_worker, rows_dev, cells), jnp.float32)
+
+    sends, = pl.pallas_call(
         functools.partial(gather_kernel, n_mem),
-        out_shape=[block] * chunks,
+        out_shape=[block],
         in_specs=[smem, whole()],
-        out_specs=[whole()] * chunks,
+        out_specs=[whole()],
         scratch_shapes=[pltpu.VMEM((cells // 128, rows_dev * band, 128), jnp.float32)],
         name="gather_patches",
     )(order, ensemble.reshape(rows_dev * band, cells))
 
-    states = [lax.all_to_all(s, "mem", split_axis=0, concat_axis=0, tiled=True) for s in sends]
-
-    spread_shape = jax.ShapeDtypeStruct((per_worker, members, members), jnp.float32)
-    spread = None
-    backs = []
-    for c in range(chunks):
-        first = c * per
-        in_specs = [
-            pl.BlockSpec((n_mem, group, rows_dev, cells), lambda i, *_: (0, i, 0, 0)),
-            whole(), whole(), whole(), whole(),
-        ]
-        operands = [worker, obs_count[0], states[c], column_operator, obs_index[0], obs_values[0], obs_precision[0]]
-        aliases = {}
-        if spread is not None:
-            in_specs.append(pl.BlockSpec(memory_space=pl.ANY))
-            operands.append(spread)
-            aliases = {7: 0}
-        base = first // group
-        spread, updated = pl.pallas_call(
-            functools.partial(analyse, group, per_worker, first),
-            out_shape=[spread_shape, block],
-            grid_spec=pltpu.PrefetchScalarGridSpec(
-                num_scalar_prefetch=2,
-                grid=(per // group,),
-                in_specs=in_specs,
-                out_specs=[
-                    pl.BlockSpec((group, members, members), lambda i, *_, base=base: (base + i, 0, 0)),
-                    pl.BlockSpec((n_mem, group, rows_dev, cells), lambda i, *_: (0, i, 0, 0)),
-                ],
-                scratch_shapes=[
-                    pltpu.VMEM((group, members, cells), jnp.float32),
-                    pltpu.VMEM((group, members, members), jnp.float32),
-                    pltpu.VMEM((group, members, members), jnp.float32),
-                    pltpu.VMEM((group, 8, members), jnp.float32),
-                ],
-            ),
-            input_output_aliases=aliases,
-            cost_estimate=pl.CostEstimate(
-                flops=per * 36 * 4 * 2 * members ** 3, transcendentals=0,
-                bytes_accessed=per * 4 * (2 * members * cells + members * members),
-            ),
-            name=f"analyse_{c}",
-        )(*operands)
-        backs.append(lax.all_to_all(updated, "mem", split_axis=0, concat_axis=0, tiled=True))
+    spread, back = pl.pallas_call(
+        functools.partial(analyse, n_mem, group),
+        out_shape=[jax.ShapeDtypeStruct((per_worker, members, members), jnp.float32), block],
+        in_specs=[smem, pl.BlockSpec(memory_space=pl.ANY), whole(), whole(), whole(), whole()],
+        out_specs=[whole(), pl.BlockSpec(memory_space=pl.ANY)],
+        scratch_shapes=[
+            pltpu.VMEM((per_worker, n_mem, rows_dev, cells), jnp.float32),
+            pltpu.VMEM((per_worker, n_mem, rows_dev, cells), jnp.float32),
+            pltpu.VMEM((group, members, cells), jnp.float32),
+            pltpu.VMEM((group, members, members), jnp.float32),
+            pltpu.VMEM((group, members, members), jnp.float32),
+            pltpu.VMEM((group, 8, members), jnp.float32),
+            pltpu.SemaphoreType.DMA(()),
+            pltpu.SemaphoreType.DMA((per_worker,)),
+            pltpu.SemaphoreType.DMA((per_worker,)),
+            pltpu.SemaphoreType.DMA(()),
+            pltpu.SemaphoreType.DMA(()),
+            pltpu.SemaphoreType.DMA((per_worker,)),
+        ],
+        compiler_params=pltpu.CompilerParams(collective_id=0, has_side_effects=True),
+        name="analyse",
+    )(obs_count[0], sends, column_operator, obs_index[0], obs_values[0], obs_precision[0])
 
     restored = pl.pallas_call(
         functools.partial(scatter_kernel, n_mem),
         out_shape=jax.ShapeDtypeStruct((rows_dev * band, cells), jnp.float32),
-        in_specs=[smem] + [whole()] * chunks,
+        in_specs=[smem] + [whole()],
         out_specs=whole(),
         scratch_shapes=[pltpu.VMEM((cells // 128, rows_dev * band, 128), jnp.float32)],
         name="restore_patches",
-    )(order, *backs)
+    )(order, back)
     return (restored.reshape(rows_dev, band, cells), spread[None])
 
 

time: 198 us -> 129 us (0.65)
  the two profiles are of different devices: /device:TPU:0 before, /device:TPU:24 now
where the time goes in v2:
time: 129 us
  Pallas kernels  127 us (98%)
  local copies, waits for them, and re-layouts  1.32 us (1%)
    pallas_call x1, Pallas kernels, local(): pl.pallas_call(functools.partial(analyse, n_mem, group), out_shape=[jax.S...  115 us
    pallas_call x1, Pallas kernels, local(): pl.pallas_call(functools.partial(gather_kernel, n_mem), out_shape=[block]...  6.12 us
    pallas_call x1, Pallas kernels, local(): pl.pallas_call(functools.partial(scatter_kernel, n_mem), out_shape=jax.Sh...  5.43 us

profile of v2, /device:TPU:24, one launch (start us, length us, event | category | flops | bytes accessed | tf_op | source)
XLA Modules:
  0.0 129.0 jit_solution(16877415134810949254)
XLA Ops:
  0.6 6.1 %gather_patches.1.sends_ref = f32[8,8,32,256]{3,2,1,0:T(8,128)} custom-call(s32[64]{0:T(128)} %bitcast.14, f32[2048,256]{1,0:T(8,128)} %bitcast.8), custom_call_target="tpu_custom_call" | custom-call | tf_op jit(solution)/shard_map/gather_patches/pallas_call | solution.py:242
  6.8 115.5 %analyse.1 = (f32[8,256,256]{2,1,0:T(8,128)}, f32[8,8,32,256]{3,2,1,0:T(8,128)}) custom-call(s32[8]{0:T(128)} %bitcast.16, f32[8,8,32,256]{3,2,1,0:T(8,128)} %gather_patches.1.sends_ref, f32[128,128]{1,0:T(8,128)} %op_ref.1, s32[64,512]{1,0:T(8,128)} %bitcast.11, f32[8,512]{1,0:T(8,128)} %bitcast.12, f32[8,512]{1,0:T(8,128)} %bitcast.13), custom_call_target="tpu_custom_call" | custom-call | tf_op jit(solution)/shard_map/analyse/pallas_call | solution.py:251
  122.2 0.0 copy-start
  122.2 5.4 %restore_patches.1 = f32[2048,256]{1,0:T(8,128)} custom-call(s32[64]{0:T(128)} %bitcast.15, f32[8,8,32,256]{3,2,1,0:T(8,128)} %get-tuple-element.4.refs_0_), custom_call_target="tpu_custom_call" | custom-call | tf_op jit(solution)/shard_map/restore_patches/pallas_call | solution.py:274
  127.7 0.0 copy-done
  127.7 1.3 %copy.10 = f32[1,8,256,256]{3,2,1,0:T(8,128)} copy(f32[1,8,256,256]{3,2,1,0:T(8,128)S(1)} %bitcast.10) | data formatting | bytes 4194304
Async XLA Ops:
  122.2 5.4 %copy-start = (f32[8,256,256]{2,1,0:T(8,128)S(1)}, f32[8,256,256]{2,1,0:T(8,128)}, u32[]{:S(2)}) copy-start(f32[8,256,256]{2,1,0:T(8,128)} %get-tuple-element.5) | copy-start | bytes 6291460

commit v3 on v2

--- a/solution.py
+++ b/solution.py
@@ -9,7 +9,7 @@
 from jax.sharding import PartitionSpec as P
 
 ITERS = 12
-LIGHT = 6
+LIGHT = 8
 MESH = pl.DeviceIdType.MESH
 HIGHEST = lax.Precision.HIGHEST
 
@@ -23,14 +23,15 @@
     return high, (x - high.astype(jnp.float32)).astype(jnp.bfloat16)
 
 
-def product(left, right, full):
+def product(left, right, full, right_dim=0):
     lh, ll = left
     rh, rl = right
     lefts = [lh, lh, ll, ll] if full else [lh, lh, ll]
     rights = [rh, rl, rh, rl] if full else [rh, rl, rh]
-    return jnp.dot(
+    return lax.dot_general(
         jnp.concatenate(lefts, axis=1),
-        jnp.concatenate(rights, axis=0),
+        jnp.concatenate(rights, axis=right_dim),
+        (((1,), (right_dim,)), ((), ())),
         preferred_element_type=jnp.float32,
     )
 
@@ -52,8 +53,8 @@
         z_ref[g] = 1.5 * z - 0.5 * product(turn, zp, full)
 
 
-def analyse(n_mem, group, count_ref, sends_ref, op_ref, index_ref, value_ref, weight_ref, spread_ref, back_ref,
-            inbox, outbox, pert_ref, y_ref, z_ref, row_ref, in_send, in_recv, own_sem, out_send, out_recv, home_sem):
+def analyse(n_mem, group, order_ref, count_ref, x_ref, op_ref, index_ref, value_ref, weight_ref, spread_ref, back_ref,
+            lanes_ref, sends_ref, inbox, outbox, pert_ref, y_ref, z_ref, col_ref, mean_ref, in_send, in_recv, own_sem, out_send, out_recv, home_sem):
     per_worker, workers, rows_dev, cells = inbox.shape
     members = workers * rows_dev
     levels = op_ref.shape[0]
@@ -66,6 +67,21 @@
 
     barrier = pltpu.get_barrier_semaphore()
     lax.fori_loop(1, n_mem, greet, 0)
+    halves, _, lanes = lanes_ref.shape
+    band = order_ref.shape[0]
+    for h in range(halves):
+        lanes_ref[h] = x_ref[:, h * lanes:(h + 1) * lanes]
+
+    def stage(i):
+        def one(w, carry):
+            q = order_ref[w * per_worker + i]
+            for h in range(halves):
+                sends_ref[w, i, :, h * lanes:(h + 1) * lanes] = lanes_ref[h, pl.ds(q, rows_dev, stride=band), :]
+            return carry
+
+        lax.fori_loop(0, n_mem, one, 0)
+
+    stage(0)
     pl.semaphore_wait(barrier, n_mem - 1)
 
     def own_in(i):
@@ -74,7 +90,7 @@
     def own_back(i):
         return pltpu.make_async_copy(outbox.at[i, me], back_ref.at[me, i], home_sem.at[i])
 
-    def issue(i, carry):
+    def issue(i):
         own_in(i).start()
 
         def one(d, carry):
@@ -87,9 +103,14 @@
             return carry
 
         lax.fori_loop(1, n_mem, one, 0)
-        return carry
-
-    lax.fori_loop(0, per_worker, issue, 0)
+
+    def feed(i, carry):
+        stage(i + 1)
+        issue(i)
+        return carry
+
+    lax.fori_loop(0, per_worker - 1, feed, 0)
+    issue(per_worker - 1)
     eye = (
         lax.broadcasted_iota(jnp.int32, (members, members), 0)
         == lax.broadcasted_iota(jnp.int32, (members, members), 1)
@@ -133,7 +154,8 @@
         pert_ref[g] = pert
         op = op_ref[...]
         columns = cells // levels
-        chan = jnp.concatenate([exact(pert[:, c * levels:(c + 1) * levels], op) for c in range(columns)], axis=1)
+        op_pieces = pieces(op)
+        chan = jnp.concatenate([product(pieces(pert[:, c * levels:(c + 1) * levels]), op_pieces, False) for c in range(columns)], axis=1)
         wide = jnp.broadcast_to(mean, (8, cells))
         chan_mean = jnp.concatenate([exact(wide[:, c * levels:(c + 1) * levels], op) for c in range(columns)], axis=1)
         width = chan.shape[1]
@@ -148,14 +170,16 @@
         left = stack - s0.astype(jnp.float32)
         s1 = left.astype(jnp.bfloat16)
         s2 = (left - s1.astype(jnp.float32)).astype(jnp.bfloat16)
-        binned = sum(
-            lax.dot_general(s, picker, (((1,), (1,)), ((), ())), preferred_element_type=jnp.float32)
-            for s in (s2, s1, s0)
+        binned = lax.dot_general(
+            jnp.concatenate([s0, s1, s2], axis=0), picker, (((1,), (1,)), ((), ())),
+            preferred_element_type=jnp.float32,
         )
+        binned = binned[0:16] + (binned[16:32] + binned[32:48])
         total = binned[0:1]
         innov = binned[1:2] - chan_mean[0:1] * total
         system = exact(chan * total, chan, 1) + jnp.where(eye, members - 1.0, 0.0)
-        row_ref[g] = exact(jnp.broadcast_to(innov, (8, width)), chan, 1)
+        col_ref[g] = jnp.sum(chan * innov, axis=1, keepdims=True)
+        mean_ref[g] = wide
         trace_value = jnp.sum(jnp.sum(jnp.where(eye, system, 0.0), axis=0, keepdims=True), axis=1, keepdims=True)
         y = system / trace_value
         yp = pieces(y)
@@ -175,10 +199,11 @@
         z = z_ref[g]
         spread = z * (math.sqrt(members - 1.0) / jnp.sqrt(trace_value))
         spread_ref[spot] = spread
-        weights = exact(exact(row_ref[g], z, 1), z, 1)[0:1] / trace_value
-        state_mean = jnp.mean(inbox[spot].reshape(members, cells), axis=0, keepdims=True)
-        coef = spread + weights
-        update = state_mean + product(pieces(coef), pieces(pert_ref[g]), False)
+        inner = jnp.sum(z * col_ref[g], axis=0, keepdims=True)
+        weights = jnp.sum(z * inner, axis=1, keepdims=True) / trace_value
+        pert = pert_ref[g]
+        shift = mean_ref[g][0:1] + jnp.sum(pert * weights, axis=0, keepdims=True)
+        update = shift + product(pieces(spread), pieces(pert), False)
         outbox[spot] = update.reshape(workers, rows_dev, cells)
 
     lax.fori_loop(0, per_worker // group, step, 0)
@@ -189,24 +214,6 @@
     pltpu.make_async_copy(posted, posted, out_recv).wait()
     for i in range(per_worker):
         own_back(i).wait()
-
-
-def gather_kernel(n_mem, order_ref, x_ref, *rest):
-    outs, lanes_ref = rest[:-1], rest[-1]
-    halves, _, lanes = lanes_ref.shape
-    for h in range(halves):
-        lanes_ref[h] = x_ref[:, h * lanes:(h + 1) * lanes]
-    band = order_ref.shape[0]
-    per = outs[0].shape[1]
-    rows = outs[0].shape[2]
-    chunks = len(outs)
-    for c, out in enumerate(outs):
-        @pl.loop(0, n_mem * per)
-        def _(t):
-            w, i = t // per, lax.rem(t, per)
-            q = order_ref[(w * chunks + c) * per + i]
-            for h in range(halves):
-                out[w, i, :, h * lanes:(h + 1) * lanes] = lanes_ref[h, pl.ds(q, rows, stride=band), :]
 
 
 def scatter_kernel(n_mem, order_ref, *refs):
@@ -239,27 +246,21 @@
     smem = pl.BlockSpec(memory_space=pltpu.SMEM)
     block = jax.ShapeDtypeStruct((n_mem, per_worker, rows_dev, cells), jnp.float32)
 
-    sends, = pl.pallas_call(
-        functools.partial(gather_kernel, n_mem),
-        out_shape=[block],
-        in_specs=[smem, whole()],
-        out_specs=[whole()],
-        scratch_shapes=[pltpu.VMEM((cells // 128, rows_dev * band, 128), jnp.float32)],
-        name="gather_patches",
-    )(order, ensemble.reshape(rows_dev * band, cells))
-
     spread, back = pl.pallas_call(
         functools.partial(analyse, n_mem, group),
         out_shape=[jax.ShapeDtypeStruct((per_worker, members, members), jnp.float32), block],
-        in_specs=[smem, pl.BlockSpec(memory_space=pl.ANY), whole(), whole(), whole(), whole()],
+        in_specs=[smem, smem, whole(), whole(), whole(), whole(), whole()],
         out_specs=[whole(), pl.BlockSpec(memory_space=pl.ANY)],
         scratch_shapes=[
+            pltpu.VMEM((cells // 128, rows_dev * band, 128), jnp.float32),
+            pltpu.VMEM((n_mem, per_worker, rows_dev, cells), jnp.float32),
             pltpu.VMEM((per_worker, n_mem, rows_dev, cells), jnp.float32),
             pltpu.VMEM((per_worker, n_mem, rows_dev, cells), jnp.float32),
             pltpu.VMEM((group, members, cells), jnp.float32),
             pltpu.VMEM((group, members, members), jnp.float32),
             pltpu.VMEM((group, members, members), jnp.float32),
-            pltpu.VMEM((group, 8, members), jnp.float32),
+            pltpu.VMEM((group, members, 1), jnp.float32),
+            pltpu.VMEM((group, 8, cells), jnp.float32),
             pltpu.SemaphoreType.DMA(()),
             pltpu.SemaphoreType.DMA((per_worker,)),
             pltpu.SemaphoreType.DMA((per_worker,)),
@@ -269,7 +270,7 @@
         ],
         compiler_params=pltpu.CompilerParams(collective_id=0, has_side_effects=True),
         name="analyse",
-    )(obs_count[0], sends, column_operator, obs_index[0], obs_values[0], obs_precision[0])
+    )(order, obs_count[0], ensemble.reshape(rows_dev * band, cells), column_operator, obs_index[0], obs_values[0], obs_precision[0])
 
     restored = pl.pallas_call(
         functools.partial(scatter_kernel, n_mem),

time: 129 us -> 112 us (0.87)
  Pallas kernels: 127 us -> 110 us
    pallas_call x1, Pallas kernels: 115 us -> 105 us  [local(): pl.pallas_call(functools.partial(analyse, n_mem, group), out_shape=[jax.S...]
    pallas_call x1 -> x0, Pallas kernels: 6.12 us -> none  [local(): pl.pallas_call(functools.partial(gather_kernel, n_mem), out_shape=[block]...]
where the time goes in v3:
time: 112 us
  Pallas kernels  110 us (98%)
  local copies, waits for them, and re-layouts  1.32 us (1%)
    pallas_call x1, Pallas kernels, local(): pl.pallas_call(functools.partial(analyse, n_mem, group), out_shape=[jax.S...  105 us
    pallas_call x1, Pallas kernels, local(): pl.pallas_call(functools.partial(scatter_kernel, n_mem), out_shape=jax.Sh...  5.43 us

profile of v3, /device:TPU:24, one launch (start us, length us, event | category | flops | bytes accessed | tf_op | source)
XLA Modules:
  0.0 112.0 jit_solution(13926212010043591206)
XLA Ops:
  0.6 104.6 %analyse.1 = (f32[8,256,256]{2,1,0:T(8,128)}, f32[8,8,32,256]{3,2,1,0:T(8,128)}) custom-call(s32[64]{0:T(128)} %bitcast.14, s32[8]{0:T(128)} %bitcast.16, f32[2048,256]{1,0:T(8,128)} %bitcast.8, f32[128,128]{1,0:T(8,128)} %op_ref.1, s32[64,512]{1,0:T(8,128)} %bitcast.11, f32[8,512]{1,0:T(8,128)} %bitcast.12, f32[8,512]{1,0:T(8,128)} %bitcast.13), custom_call_target="tpu_custom_call" | custom-call | tf_op jit(solution)/shard_map/analyse/pallas_call | solution.py:249
  105.2 0.0 copy-start
  105.2 5.4 %restore_patches.1 = f32[2048,256]{1,0:T(8,128)} custom-call(s32[64]{0:T(128)} %bitcast.15, f32[8,8,32,256]{3,2,1,0:T(8,128)} %get-tuple-element.4.refs_0_), custom_call_target="tpu_custom_call" | custom-call | tf_op jit(solution)/shard_map/restore_patches/pallas_call | solution.py:275
  110.6 0.0 copy-done
  110.6 1.3 %copy.10 = f32[1,8,256,256]{3,2,1,0:T(8,128)} copy(f32[1,8,256,256]{3,2,1,0:T(8,128)S(1)} %bitcast.10) | data formatting | bytes 4194304
Async XLA Ops:
  105.2 5.4 %copy-start = (f32[8,256,256]{2,1,0:T(8,128)S(1)}, f32[8,256,256]{2,1,0:T(8,128)}, u32[]{:S(2)}) copy-start(f32[8,256,256]{2,1,0:T(8,128)} %get-tuple-element.5) | copy-start | bytes 6291460

commit v4 on v3

--- a/solution.py
+++ b/solution.py
@@ -116,22 +116,27 @@
         == lax.broadcasted_iota(jnp.int32, (members, members), 1)
     )
 
-    def step(t, carry):
-        for g in range(group):
-            spot = t * group + g
-            own_in(spot).wait()
-            arrived = inbox.at[spot, pl.ds(0, n_mem - 1)]
-            pltpu.make_async_copy(arrived, arrived, in_recv.at[spot]).wait()
-        scales = []
-        for g in range(group):
-            scales.append(prepare(t * group + g, g))
+    def run(base, size):
+        for g in range(size):
+            own_in(base + g).wait()
+            arrived = inbox.at[base + g, pl.ds(0, n_mem - 1)]
+            pltpu.make_async_copy(arrived, arrived, in_recv.at[base + g]).wait()
+        scales = [prepare(base + g, g) for g in range(size)]
+
+        def light(k, carry):
+            sweep(y_ref, z_ref, size, False, False)
+            return carry
+
+        def firm(k, carry):
+            sweep(y_ref, z_ref, size, True, False)
+            return carry
+
         lax.fori_loop(1, LIGHT, light, 0)
         lax.fori_loop(LIGHT, ITERS - 1, firm, 0)
-        sweep(y_ref, z_ref, group, True, True)
-        for g in range(group):
-            finish(t * group + g, g, scales[g])
-            launch(t * group + g)
-        return carry
+        sweep(y_ref, z_ref, size, True, True)
+        for g in range(size):
+            finish(base + g, g, scales[g])
+            launch(base + g)
 
     def launch(spot):
         own_back(spot).start()
@@ -187,14 +192,6 @@
         y_ref[g] = 1.5 * y - 0.5 * product(yp, yp, False)
         return trace_value
 
-    def light(k, carry):
-        sweep(y_ref, z_ref, group, False, False)
-        return carry
-
-    def firm(k, carry):
-        sweep(y_ref, z_ref, group, True, False)
-        return carry
-
     def finish(spot, g, trace_value):
         z = z_ref[g]
         spread = z * (math.sqrt(members - 1.0) / jnp.sqrt(trace_value))
@@ -206,7 +203,18 @@
         update = shift + product(pieces(spread), pieces(pert), False)
         outbox[spot] = update.reshape(workers, rows_dev, cells)
 
-    lax.fori_loop(0, per_worker // group, step, 0)
+    edge = 1 if group > 1 and per_worker % group == 0 and per_worker > group else 0
+    middle = (per_worker - 2 * edge) // group
+
+    def step(t, carry):
+        run(edge + t * group, group)
+        return carry
+
+    if edge:
+        run(0, 1)
+    lax.fori_loop(0, middle, step, 0)
+    if edge:
+        run(per_worker - 1, 1)
     sent = sends_ref.at[pl.ds(0, n_mem - 1)]
     pltpu.make_async_copy(sent, sent, in_send).wait()
     posted = back_ref.at[pl.ds(0, n_mem - 1)]

time: 112 us -> 109 us (0.973)
  Pallas kernels: 110 us -> 107 us
    pallas_call x1, Pallas kernels: 105 us -> 102 us  [local(): pl.pallas_call(functools.partial(analyse, n_mem, group), out_shape=[jax.S...]
where the time goes in v4:
time: 109 us
  Pallas kernels  107 us (98%)
  local copies, waits for them, and re-layouts  1.32 us (1%)
    pallas_call x1, Pallas kernels, local(): pl.pallas_call(functools.partial(analyse, n_mem, group), out_shape=[jax.S...  102 us
    pallas_call x1, Pallas kernels, local(): pl.pallas_call(functools.partial(scatter_kernel, n_mem), out_shape=jax.Sh...  5.43 us

profile of v4, /device:TPU:24, one launch (start us, length us, event | category | flops | bytes accessed | tf_op | source)
XLA Modules:
  0.0 109.1 jit_solution(2463080982122293579)
XLA Ops:
  0.6 101.7 %analyse.1 = (f32[8,256,256]{2,1,0:T(8,128)}, f32[8,8,32,256]{3,2,1,0:T(8,128)}) custom-call(s32[64]{0:T(128)} %bitcast.14, s32[8]{0:T(128)} %bitcast.16, f32[2048,256]{1,0:T(8,128)} %bitcast.8, f32[128,128]{1,0:T(8,128)} %op_ref.1, s32[64,512]{1,0:T(8,128)} %bitcast.11, f32[8,512]{1,0:T(8,128)} %bitcast.12, f32[8,512]{1,0:T(8,128)} %bitcast.13), custom_call_target="tpu_custom_call" | custom-call | tf_op jit(solution)/shard_map/analyse/pallas_call | solution.py:257
  102.4 0.0 copy-start
  102.4 5.4 %restore_patches.1 = f32[2048,256]{1,0:T(8,128)} custom-call(s32[64]{0:T(128)} %bitcast.15, f32[8,8,32,256]{3,2,1,0:T(8,128)} %get-tuple-element.4.refs_0_), custom_call_target="tpu_custom_call" | custom-call | tf_op jit(solution)/shard_map/restore_patches/pallas_call | solution.py:283
  107.8 0.0 copy-done
  107.8 1.3 %copy.10 = f32[1,8,256,256]{3,2,1,0:T(8,128)} copy(f32[1,8,256,256]{3,2,1,0:T(8,128)S(1)} %bitcast.10) | data formatting | bytes 4194304
Async XLA Ops:
  102.4 5.4 %copy-start = (f32[8,256,256]{2,1,0:T(8,128)S(1)}, f32[8,256,256]{2,1,0:T(8,128)}, u32[]{:S(2)}) copy-start(f32[8,256,256]{2,1,0:T(8,128)} %get-tuple-element.5) | copy-start | bytes 6291460

commit v5 on v4

--- a/solution.py
+++ b/solution.py
@@ -232,7 +232,7 @@
     rows = ins[0].shape[2]
     chunks = len(ins)
     for c, block in enumerate(ins):
-        @pl.loop(0, n_mem * per)
+        @pl.loop(0, n_mem * per, unroll=8)
         def _(t):
             w, i = t // per, lax.rem(t, per)
             q = order_ref[(w * chunks + c) * per + i]

time: 109 us -> 109 us (level)
  no operation moved by 1% of the time
where the time goes in v5:
time: 109 us
  Pallas kernels  107 us (98%)
  local copies, waits for them, and re-layouts  1.32 us (1%)
    pallas_call x1, Pallas kernels, local(): pl.pallas_call(functools.partial(analyse, n_mem, group), out_shape=[jax.S...  102 us
    pallas_call x1, Pallas kernels, local(): pl.pallas_call(functools.partial(scatter_kernel, n_mem), out_shape=jax.Sh...  5.37 us

profile of v5, /device:TPU:24, one launch (start us, length us, event | category | flops | bytes accessed | tf_op | source)
XLA Modules:
  0.0 109.1 jit_solution(2758836250939746968)
XLA Ops:
  0.6 101.7 %analyse.1 = (f32[8,256,256]{2,1,0:T(8,128)}, f32[8,8,32,256]{3,2,1,0:T(8,128)}) custom-call(s32[64]{0:T(128)} %bitcast.14, s32[8]{0:T(128)} %bitcast.16, f32[2048,256]{1,0:T(8,128)} %bitcast.8, f32[128,128]{1,0:T(8,128)} %op_ref.1, s32[64,512]{1,0:T(8,128)} %bitcast.11, f32[8,512]{1,0:T(8,128)} %bitcast.12, f32[8,512]{1,0:T(8,128)} %bitcast.13), custom_call_target="tpu_custom_call" | custom-call | tf_op jit(solution)/shard_map/analyse/pallas_call | solution.py:257
  102.4 0.0 copy-start
  102.4 5.4 %restore_patches.1 = f32[2048,256]{1,0:T(8,128)} custom-call(s32[64]{0:T(128)} %bitcast.15, f32[8,8,32,256]{3,2,1,0:T(8,128)} %get-tuple-element.4.refs_0_), custom_call_target="tpu_custom_call" | custom-call | tf_op jit(solution)/shard_map/restore_patches/pallas_call | solution.py:283
  107.8 0.0 copy-done
  107.8 1.3 %copy.10 = f32[1,8,256,256]{3,2,1,0:T(8,128)} copy(f32[1,8,256,256]{3,2,1,0:T(8,128)S(1)} %bitcast.10) | data formatting | bytes 4194304
Async XLA Ops:
  102.4 5.4 %copy-start = (f32[8,256,256]{2,1,0:T(8,128)S(1)}, f32[8,256,256]{2,1,0:T(8,128)}, u32[]{:S(2)}) copy-start(f32[8,256,256]{2,1,0:T(8,128)} %get-tuple-element.5) | copy-start | bytes 6291460
